TPU v7x, 256 devices: a whole 4x4x8 slice. The times are simulated.
256 devices in a mesh: row: 16 (over z, y_lo), col: 16 (over x, y_hi, core).
Axes of the slice: x: 4, y: 4 (y_hi: 2, y_lo: 2; y = y_hi * 2 + y_lo), z: 8, core: 2. Of those that a mesh axis runs over, the one named last changes fastest.
Arguments:
- velocity: float32 [3, 128, 256, 1024], P(None, 'col', 'row'), may hold values from -6 to 6
- derivative_x: float32 [1024, 1024], replicated, may hold values from -4 to 4, as said below
- derivative_y: float32 [256, 256], replicated, may hold values from -4 to 4, as said below
- derivative_z: float32 [128, 128], replicated, may hold values from -4 to 4, as said below
- smoothing_x: float32 [1024, 1024], replicated, may hold values from -2 to 2, as said below
- smoothing_y: float32 [256, 256], replicated, may hold values from -2 to 2, as said below
- smoothing_z: float32 [128, 128], replicated, may hold values from -2 to 2, as said below
Outputs:
- filtered_velocity: float32 [3, 128, 256, 1024], P(None, 'col', 'row')
Inputs may be any that keep to these rules, and one draw needn't show every extreme that they name: derivative_x is diag(m) times the inverse of the periodic tridiagonal matrix with 1 on the diagonal and 9/20 beside it, times the periodic stencil 63/80 (f[i+1] - f[i-1]) + 9/100 (f[i+2] - f[i-2]) - 7/1200 (f[i+3] - f[i-3]); m holds one positive metric factor per grid line. `derivative_y`: as derivative_x, for the y lines. smoothing_x is the inverse of the periodic tridiagonal matrix with 1 on the diagonal and a[i] beside it in row i, times the periodic filter stencil of row i, whose weights are: at offset 0, 11/16 plus 5/8 times a[i]; at offsets -1 and 1 each, 15/64 plus 17/32 times a[i]; at offsets -2 and 2 each, -3/32 plus 3/16 times a[i]; at offsets -3 and 3 each, 1/64 minus 1/32 times a[i]; each a[i] lies in 0.44 to 0.499. `derivative_z`: as derivative_x, for the z lines. `smoothing_y`: as smoothing_x, for the y lines. `smoothing_z`: as smoothing_x, for the z lines.
All inputs are finite; a program needn't handle non-finite values.
Results may differ from a plain program's by a relative error of at most 0.000082.
Values sent between devices are 32-bit elements; how exact they have to be, the bound alone decides.
A program may use at most 64 MiB of HBM per device.

v0:
```python
import jax
import jax.numpy as jnp
from jax import lax
from jax.sharding import PartitionSpec as P


def along_last(matrix, volume):
    return lax.dot_general(
        volume, matrix, (((3,), (1,)), ((), ())), precision=lax.Precision.HIGHEST
    )


def along_lines(matrix, volume):
    return jnp.dot(matrix, volume, precision=lax.Precision.HIGHEST)


def times_component(volume, component, outer_count):
    line_count = volume.shape[0]
    grouped = volume.reshape(line_count, outer_count, 3, -1)
    return (grouped * grouped[:, :, component : component + 1]).reshape(line_count, -1)


def swap_lines(volume, groups, inner_count, narrow):
    line_count = volume.shape[0]
    local_lines = line_count // groups
    grouped = volume.reshape(groups, local_lines, 3, inner_count, narrow)
    grouped = jnp.transpose(grouped, (3, 0, 2, 1, 4))
    return grouped.reshape(inner_count, groups, 3 * local_lines * narrow)


def pair_to_y(leading, second, num_row, rows_y, narrow):
    sent = (
        lax.all_to_all(
            swap_lines(leading, num_row, rows_y, narrow),
            "row",
            split_axis=1,
            concat_axis=0,
            tiled=True,
        ),
        lax.all_to_all(
            swap_lines(second, num_row, rows_y, narrow),
            "row",
            split_axis=1,
            concat_axis=0,
            tiled=True,
        ),
    )
    total_y = rows_y * num_row
    return (sent[0].reshape(total_y, -1), sent[1].reshape(total_y, -1))


def single_to_z(volume, num_row, rows_z, narrow):
    sent = lax.all_to_all(
        swap_lines(volume, num_row, rows_z, narrow), "row", split_axis=1, concat_axis=0, tiled=True
    )
    return sent.reshape(rows_z * num_row, -1)


def finish_x(matrix, volume, slab_z, rows_y):
    result = lax.dot_general(
        volume, matrix, (((0,), (1,)), ((), ())), precision=lax.Precision.HIGHEST
    )
    return result.reshape(3, slab_z, rows_y, matrix.shape[0])


def on_device(
    velocity, derivative_x, derivative_y, derivative_z, smoothing_x, smoothing_y, smoothing_z
):
    num_row = lax.axis_size("row")
    num_col = lax.axis_size("col")
    count_c, slab_z, rows_y, width_x = velocity.shape
    total_z = slab_z * num_col
    rows_z = total_z // num_row
    narrow = width_x // num_col
    tendency = -along_last(derivative_x, velocity * velocity[0:1])

    def to_z_lines(volume):
        grouped = volume.reshape(count_c, slab_z, rows_y, num_col, narrow)
        return jnp.transpose(grouped, (1, 3, 0, 2, 4)).reshape(slab_z, num_col, -1)

    flow_z, tend_z = (
        lax.all_to_all(to_z_lines(velocity), "col", split_axis=1, concat_axis=0, tiled=True),
        lax.all_to_all(to_z_lines(tendency), "col", split_axis=1, concat_axis=0, tiled=True),
    )
    flow_z = flow_z.reshape(total_z, -1)
    tend_z = tend_z.reshape(total_z, -1)
    tend_z = tend_z - along_lines(derivative_z, times_component(flow_z, 2, 1))
    flow_y, tend_y = pair_to_y(flow_z, tend_z, num_row, rows_y, narrow)
    tend_y = tend_y - along_lines(derivative_y, times_component(flow_y, 1, 1))
    advanced = flow_y + 0.1 * tend_y
    smooth = along_lines(smoothing_y, advanced)
    smooth = single_to_z(smooth, num_row, rows_z, narrow)
    smooth = along_lines(smoothing_z, smooth)
    grouped = smooth.reshape(num_col, slab_z, count_c, rows_y, narrow)
    grouped = jnp.transpose(grouped, (4, 0, 2, 1, 3)).reshape(narrow, num_col, -1)
    smooth = lax.all_to_all(grouped, "col", split_axis=1, concat_axis=0, tiled=True)
    smooth = smooth.reshape(width_x, -1)
    return finish_x(smoothing_x, smooth, slab_z, rows_y)


def solution(mesh):
    in_specs = (P(None, "col", "row", None), P(), P(), P(), P(), P(), P())
    out_specs = P(None, "col", "row", None)
    return jax.shard_map(
        on_device, mesh=mesh, in_specs=in_specs, out_specs=out_specs, check_vma=False
    )
```

profile of v0, /device:TPU:1, one launch (start us, length us, event | category | flops | bytes accessed | tf_op | source)
XLA Modules:
  0.0 310.6 jit_solution(4041956890969334784)
XLA Ops:
  1.1 8.5 %fusion.11 = f32[3,8,16,1024]{3,2,1,0:T(8,128)} fusion(f32[1024,1024]{1,0:T(8,128)} %param.8, f32[3,8,16,1024]{3,2,1,0:T(8,128)} %param.7, f32[8,16,1024]{2,1,0:T(8,128)S(1)} %slice_bitcast_fusion), kind=kOutput, calls=%fused_computation.19 | convolution fusion | flops 4832624640 | bytes 7864320 | tf_op jit(solution)/shard_map/dot_general | solution.py:8
  9.6 2.5 reshape.78
  12.1 2.6 copy.88
  14.7 2.3 reshape.79
  17.1 2.1 copy.59
  19.1 8.6 %all-to-all-start.2 = ((f32[8,16,3072]{2,0,1:T(8,128)}), f32[8,16,3072]{2,0,1:T(8,128)}, u32[]{:S(2)}, u32[]{:S(2)}) async-start(f32[8,16,3072]{2,0,1:T(8,128)} %copy.59), calls=%async_computation.2 | async-start | bytes 3145728 | tf_op jit(solution)/shard_map/all_to_all | solution.py:83
  27.7 2.1 reshape.74
  29.8 2.8 copy.90
  32.6 1.8 reshape.75
  34.4 3.5 %copy.55 = f32[8,16,3072]{2,0,1:T(8,128)} copy(f32[8,16,3072]{2,1,0:T(8,128)} %reshape.75) | data formatting | bytes 3145728 | tf_op jit(solution)/shard_map/reshape | solution.py:79
  37.9 12.7 %all-to-all-done.2 = f32[8,16,3072]{2,0,1:T(8,128)} async-done(((f32[8,16,3072]{2,0,1:T(8,128)}), f32[8,16,3072]{2,0,1:T(8,128)}, u32[]{:S(2)}, u32[]{:S(2)}) %all-to-all-start.2) | async-done | bytes 1572896 | tf_op jit(solution)/shard_map/all_to_all | solution.py:83
  50.6 4.8 %all-to-all-start = ((f32[8,16,3072]{2,0,1:T(8,128)}), f32[8,16,3072]{2,0,1:T(8,128)S(1)}, u32[]{:S(2)}, u32[]{:S(2)}) async-start(f32[8,16,3072]{2,0,1:T(8,128)} %copy.55), calls=%async_computation | async-start | bytes 3145728 | tf_op jit(solution)/shard_map/all_to_all | solution.py:82
  55.5 3.0 copy.62
  58.5 19.8 %all-to-all-done = f32[8,16,3072]{2,0,1:T(8,128)S(1)} async-done(((f32[8,16,3072]{2,0,1:T(8,128)}), f32[8,16,3072]{2,0,1:T(8,128)S(1)}, u32[]{:S(2)}, u32[]{:S(2)}) %all-to-all-start) | async-done | bytes 1572896 | tf_op jit(solution)/shard_map/all_to_all | solution.py:82
  78.3 2.2 reshape_reshape.13
  80.5 2.1 slice.12
  84.9 1.6 copy.61
  86.5 4.5 %fusion.4 = f32[128,3072]{0,1:T(8,128)S(1)} fusion(f32[128,3072]{0,1:T(8,128)} %copy.62, f32[128,128]{1,0:T(8,128)S(1)} %copy-done.3, f32[128,3072]{1,0:T(8,128)} %copy.61, f32[8,16,3072]{2,0,1:T(8,128)S(1)} %all-to-all-done), kind=kOutput, calls=%fused_computation.6 | convolution fusion | flops 604766208 | bytes 6356992 | tf_op jit(solution)/shard_map/dot_general | solution.py:14
  91.0 1.6 copy.63
  92.6 3.2 %reshape.81 = f32[16,8,3,16,64]{4,3,2,1,0:T(8,128)} reshape(f32[128,3072]{1,0:T(8,128)} %copy.63) | data formatting | bytes 3145728 | tf_op jit(solution)/shard_map/reshape | solution.py:26
  95.8 4.5 %copy.80 = f32[16,16,3,8,64]{4,3,2,0,1:T(8,128)} copy(f32[16,16,3,8,64]{4,0,2,3,1:T(8,128)} %bitcast.127) | data formatting | bytes 3145728 | tf_op jit(solution)/shard_map/reshape | solution.py:28
  100.3 3.6 %reshape.92 = f32[16,16,1536]{2,0,1:T(8,128)} reshape(f32[16,16,3,8,64]{4,3,2,0,1:T(8,128)} %copy.80) | data formatting | bytes 3145728 | tf_op jit(solution)/shard_map/reshape | solution.py:28
  103.9 8.4 %all-to-all-start.3 = ((f32[16,16,1536]{2,0,1:T(8,128)}), f32[16,16,1536]{2,0,1:T(8,128)}, u32[]{:S(2)}, u32[]{:S(2)}) async-start(f32[16,16,1536]{2,0,1:T(8,128)} %reshape.92), calls=%async_computation.3 | async-start | bytes 3145728 | tf_op jit(solution)/shard_map/all_to_all | solution.py:40
  112.4 2.1 reshape_reshape.11
  114.5 2.9 copy.89
  117.4 1.7 reshape.76
  119.0 3.5 %copy.57 = f32[16,16,1536]{2,0,1:T(8,128)} copy(f32[16,16,1536]{2,1,0:T(8,128)} %reshape.76) | data formatting | bytes 3145728 | tf_op jit(solution)/shard_map/reshape | solution.py:28
  122.5 25.7 %all-to-all-done.3 = f32[16,16,1536]{2,0,1:T(8,128)} async-done(((f32[16,16,1536]{2,0,1:T(8,128)}), f32[16,16,1536]{2,0,1:T(8,128)}, u32[]{:S(2)}, u32[]{:S(2)}) %all-to-all-start.3) | async-done | bytes 1572896 | tf_op jit(solution)/shard_map/all_to_all | solution.py:40
  148.3 7.1 %all-to-all-start.1 = ((f32[16,16,1536]{2,0,1:T(8,128)}), f32[16,16,1536]{2,0,1:T(8,128)S(1)}, u32[]{:S(2)}, u32[]{:S(2)}) async-start(f32[16,16,1536]{2,0,1:T(8,128)} %copy.57), calls=%async_computation.1 | async-start | bytes 3145728 | tf_op jit(solution)/shard_map/all_to_all | solution.py:33
  155.4 3.0 copy.68
  158.4 32.7 %all-to-all-done.1 = f32[16,16,1536]{2,0,1:T(8,128)S(1)} async-done(((f32[16,16,1536]{2,0,1:T(8,128)}), f32[16,16,1536]{2,0,1:T(8,128)S(1)}, u32[]{:S(2)}, u32[]{:S(2)}) %all-to-all-start.1) | async-done | bytes 1572896 | tf_op jit(solution)/shard_map/all_to_all | solution.py:33
  191.1 1.6 copy.69
  192.7 2.2 reshape_reshape.14
  194.9 2.1 slice.13
  199.4 1.6 copy.67
  201.0 5.2 %fusion.7 = f32[256,1536]{0,1:T(8,128)S(1)} fusion(f32[256,1536]{0,1:T(8,128)} %copy.69, f32[256,1536]{0,1:T(8,128)} %copy.68, f32[256,256]{1,0:T(8,128)S(1)} %copy-done, f32[256,1536]{1,0:T(8,128)S(1)} %bitcast.124, f32[256,1536]{1,0:T(8,128)} %copy.67), kind=kOutput, calls=%fused_computation.14 | convolution fusion | flops 1209532416 | bytes 8126464 | tf_op jit(solution)/shard_map/dot_general | solution.py:14
  207.6 1.6 copy.70
  209.3 2.4 reshape.84
  211.7 2.2 copy.82
  213.9 2.3 reshape.93
  216.2 45.3 %all_to_all.90 = f32[8,16,3072]{2,0,1:T(8,128)S(1)} all-to-all(f32[8,16,3072]{2,0,1:T(8,128)S(1)} %reshape.93), channel_id=1, replica_groups=mesh['row'=16,'col'=16] {'row'}, dimensions={1} | all-to-all | bytes 3145728 | tf_op jit(solution)/shard_map/all_to_all | solution.py:53
  261.5 2.6 convolution_bitcast_fusion
  264.2 1.6 copy.73
  265.8 2.0 reshape.87
  267.8 2.0 copy.74
  269.8 2.3 copy.75
  272.1 30.1 %all_to_all.91 = f32[64,16,384]{2,0,1:T(8,128)S(1)} all-to-all(f32[64,16,384]{2,0,1:T(8,128)S(1)} %copy.75), channel_id=1, replica_groups=mesh['row'=16,'col'=16] {'col'}, dimensions={1} | all-to-all | bytes 3145728 | tf_op jit(solution)/shard_map/all_to_all | solution.py:96
  302.7 7.9 %fusion = f32[3,8,16,1024]{3,2,1,0:T(8,128)} fusion(f32[3,8,16,1024]{3,2,1,0:T(8,128)S(1)} %bitcast.135, f32[1024,1024]{1,0:T(8,128)} %param.11), kind=kOutput, calls=%fused_computation | convolution fusion | flops 4831838208 | bytes 7340032 | tf_op jit(solution)/shard_map/dot_general | solution.py:60
  (17 shorter events, 7.6 us)
Async XLA Ops:
  0.0 201.0 %copy-start = (f32[256,256]{1,0:T(8,128)S(1)}, f32[256,256]{1,0:T(8,128)}, u32[]{:S(2)}) copy-start(f32[256,256]{1,0:T(8,128)} %param.9) | copy-start | bytes 786436
  19.1 8.6 %copy-start.1 = (f32[3,8,16,1024]{3,2,1,0:T(8,128)S(1)}, f32[3,8,16,1024]{3,2,1,0:T(8,128)}, u32[]{:S(2)}) copy-start(f32[3,8,16,1024]{3,2,1,0:T(8,128)} %param.7) | copy-start | bytes 4718596
  19.1 31.5 %all-to-all-start.2 = ((f32[8,16,3072]{2,0,1:T(8,128)}), f32[8,16,3072]{2,0,1:T(8,128)}, u32[]{:S(2)}, u32[]{:S(2)}) async-start(f32[8,16,3072]{2,0,1:T(8,128)} %copy.59), calls=%async_computation.2 | async-start | bytes 3145728 | tf_op jit(solution)/shard_map/all_to_all | solution.py:83
  50.6 27.6 %all-to-all-start = ((f32[8,16,3072]{2,0,1:T(8,128)}), f32[8,16,3072]{2,0,1:T(8,128)S(1)}, u32[]{:S(2)}, u32[]{:S(2)}) async-start(f32[8,16,3072]{2,0,1:T(8,128)} %copy.55), calls=%async_computation | async-start | bytes 3145728 | tf_op jit(solution)/shard_map/all_to_all | solution.py:82
  84.8 1.7 copy-start.3
  103.9 44.3 %all-to-all-start.3 = ((f32[16,16,1536]{2,0,1:T(8,128)}), f32[16,16,1536]{2,0,1:T(8,128)}, u32[]{:S(2)}, u32[]{:S(2)}) async-start(f32[16,16,1536]{2,0,1:T(8,128)} %reshape.92), calls=%async_computation.3 | async-start | bytes 3145728 | tf_op jit(solution)/shard_map/all_to_all | solution.py:40
  148.3 42.8 %all-to-all-start.1 = ((f32[16,16,1536]{2,0,1:T(8,128)}), f32[16,16,1536]{2,0,1:T(8,128)S(1)}, u32[]{:S(2)}, u32[]{:S(2)}) async-start(f32[16,16,1536]{2,0,1:T(8,128)} %copy.57), calls=%async_computation.1 | async-start | bytes 3145728 | tf_op jit(solution)/shard_map/all_to_all | solution.py:33
  201.0 5.2 %copy-start.2 = (f32[256,256]{1,0:T(8,128)S(1)}, f32[256,256]{1,0:T(8,128)}, u32[]{:S(2)}) copy-start(f32[256,256]{1,0:T(8,128)} %param.12) | copy-start | bytes 786436
  216.2 45.3 %copy-start.4 = (f32[128,128]{1,0:T(8,128)S(1)}, f32[128,128]{1,0:T(8,128)}, u32[]{:S(2)}) copy-start(f32[128,128]{1,0:T(8,128)} %param.13) | copy-start | bytes 196612
where the time goes:
time: 312 us; the launch traced here: 311 us
  waiting for transfers between devices  91 us (29%)
  local copies, waits for them, and re-layouts  85 us (27%)
  blocking collectives  75.4 us (24%)
  matrix products  30.1 us (10%)
  starting transfers between devices  28.9 us (9%)
    all_to_all x1, blocking collectives, single_to_z(): lax.all_to_all(swap_lines(volume, num_row, rows_z, narrow), 'row', split_...  45.3 us
    all_to_all x1, waiting for transfers between devices, pair_to_y(): lax.all_to_all(swap_lines(leading, num_row, rows_y, narrow), 'row', split...  32.7 us
    all_to_all x1, blocking collectives, on_device(): lax.all_to_all(grouped, 'col', split_axis=1, concat_axis=0, tiled=True)  30.1 us
    all_to_all x1, waiting for transfers between devices, pair_to_y(): lax.all_to_all(swap_lines(second, num_row, rows_y, narrow), 'row', split_...  25.7 us
    all_to_all x1, waiting for transfers between devices, on_device(): lax.all_to_all(to_z_lines(velocity), 'col', split_axis=1, concat_axis=0,...  19.8 us
    reshape x6, local copies, waits for them, and re-layouts, swap_lines(): return grouped.reshape(inner_count, groups, 3 * local_lines * narrow)  17.8 us
    dot_general x4, matrix products, along_lines(): return jnp.dot(matrix, volume, precision=lax.Precision.HIGHEST)  13.7 us
    all_to_all x1, waiting for transfers between devices, on_device(): lax.all_to_all(to_z_lines(tendency), 'col', split_axis=1, concat_axis=0,...  12.7 us
  transfers between devices with their start and end apart: 4, of which 4 were waited for; matrix products, arithmetic and copies ran while one was open for 8% of the time, Pallas kernels for 0%

commit v1 on v0

v1 whole, which is shorter than its diff:
```python
import functools

import jax
import jax.numpy as jnp
import numpy as np
from jax import lax
from jax.experimental import pallas as pl
from jax.experimental.pallas import tpu as pltpu
from jax.sharding import Mesh
from jax.sharding import PartitionSpec as P

AXES = ("z", "ylo", "x", "yhi", "core")
SIZES = (8, 2, 4, 2, 2)
MESH = pl.DeviceIdType.MESH
HIGHEST = lax.Precision.HIGHEST
F32 = jnp.float32
BLK = 32
NBY, NBZ, NBX = 8, 4, 8
ORDER = (1, 2, 0)
SIDE = 9.0 / 20.0
STENCIL = (63.0 / 80.0, 9.0 / 100.0, -7.0 / 1200.0)


def tridiagonal_tables(side, count):
    piv, cp = np.zeros(count), np.zeros(count)
    before = 0.0
    for i in range(count):
        piv[i] = 1.0 / (1.0 - side * before)
        before = cp[i] = side * piv[i]
    first, last = np.zeros(count), np.zeros(count)
    first[0] = cp[0]
    for i in range(1, count):
        first[i] = -cp[i] * first[i - 1]
    last[-1] = cp[-1]
    for i in range(count - 2, -1, -1):
        first[i] -= cp[i] * first[i + 1]
        last[i] = -cp[i] * last[i + 1]
    return np.stack([piv, cp, first, last])


def reduced_inverse(table, blocks):
    first, last = table[2], table[3]
    full = np.eye(16)
    for i in range(blocks):
        before, after = 8 + (i - 1) % blocks, (i + 1) % blocks
        full[i, before] += first[0]
        full[i, after] += last[0]
        full[8 + i, before] += first[-1]
        full[8 + i, after] += last[-1]
    return np.linalg.inv(full)


def lanes(array):
    return np.broadcast_to(np.asarray(array, np.float32)[..., None], array.shape + (128,))


def pade_off_diagonal(count):
    left = np.eye(count) + SIDE * (np.roll(np.eye(count), 1, 1) + np.roll(np.eye(count), -1, 1))
    right = sum(
        w * (np.roll(np.eye(count), k + 1, 1) - np.roll(np.eye(count), -k - 1, 1))
        for k, w in enumerate(STENCIL)
    )
    return float(np.linalg.solve(left, right)[0, 1])


def outside_profile():
    inner = 122
    matrix = np.eye(inner) + SIDE * (np.eye(inner, k=1) + np.eye(inner, k=-1))
    profile = np.zeros((8, 128))
    for e, row in enumerate((0, 1, 2, 125, 126, 127)):
        profile[e, row] = 1.0
    unit = np.zeros(inner)
    unit[0] = -SIDE
    profile[2, 3:125] = np.linalg.solve(matrix, unit)
    profile[3, 3:125] = np.linalg.solve(matrix, unit[::-1])
    return profile


def iota(shape, dim):
    return lax.broadcasted_iota(jnp.int32, shape, dim)


def wrapped_offset(shape, first_row, count):
    offset = iota(shape, 1) - iota(shape, 0) - first_row
    return jnp.where(offset < 0, offset + count, offset)


def metric_rows(matrix_ref, first_row, count, unit):
    block = matrix_ref[pl.ds(first_row, BLK), :]
    offset = wrapped_offset(block.shape, first_row, count)
    weight = jnp.where(offset == 1, 0.5 / unit, jnp.where(offset == count - 1, -0.5 / unit, 0.0))
    return jnp.broadcast_to(jnp.sum(block * weight, axis=1, keepdims=True), (BLK, 128))


def filter_slack(matrix_ref, count):
    shape = (count, count)
    offset = wrapped_offset(shape, 0, count)
    change = matrix_ref[...] - jnp.where(offset == 0, 1.0, 0.0)
    around = 0.5 * (pltpu.roll(change, 1, 0) + pltpu.roll(change, count - 1, 0))
    sixth = jnp.zeros(shape, F32)
    for k, w in enumerate((-20.0, 15.0, -6.0, 1.0)):
        sixth = jnp.where((offset == k) | (offset == (count - k) % count), w / 64.0, sixth)
    basis = sixth + around
    top = jnp.sum((change + around) * basis, axis=1, keepdims=True)
    return top / jnp.sum(basis * basis, axis=1, keepdims=True)


def block_tables(slack_ref, all_ref):
    def side(i):
        return 0.5 - 0.5 * slack_ref[pl.ds(i, 8, stride=BLK), :]

    def forward(i, carry):
        before, first = carry
        a = side(i)
        piv = 1.0 / (1.0 - a * before)
        cp = a * piv
        first = jnp.where(i == 0, cp, -cp * first)
        all_ref[0, i] = piv
        all_ref[1, i] = cp
        all_ref[2, i] = first
        return cp, first

    zero = jnp.zeros((8, 128), F32)
    lax.fori_loop(0, BLK, forward, (zero, zero))

    def backward(k, carry):
        first, last = carry
        i = BLK - 1 - k
        cp = all_ref[1, i]
        first = all_ref[2, i] - cp * first
        last = jnp.where(k == 0, cp, -cp * last)
        all_ref[2, i] = first
        all_ref[3, i] = last
        return first, last

    lax.fori_loop(0, BLK, backward, (zero, zero))


def invert_reduced(all_ref, blocks, out_ref):
    sub, lane = iota((8, 128), 0), iota((8, 128), 1)
    before = 8 + jnp.where(sub == 0, blocks - 1, sub - 1)
    after = jnp.where(sub == blocks - 1, 0, sub + 1)
    valid = sub < blocks

    def rows(own, first, last):
        value = jnp.where(lane == own, 1.0, 0.0)
        value += jnp.where(valid & (lane == before), first, 0.0)
        return value + jnp.where(valid & (lane == after), last, 0.0)

    full = jnp.concatenate(
        [
            rows(sub, all_ref[2, 0], all_ref[3, 0]),
            rows(8 + sub, all_ref[2, BLK - 1], all_ref[3, BLK - 1]),
        ],
        axis=0,
    )
    sub, lane = iota((16, 128), 0), iota((16, 128), 1)
    full += jnp.where(lane == 16 + sub, 1.0, 0.0)

    def eliminate(k, full):
        column = jnp.sum(jnp.where(lane == k, full, 0.0), axis=1, keepdims=True)
        row = jnp.sum(jnp.where(sub == k, full, 0.0), axis=0, keepdims=True)
        pivot = jnp.sum(jnp.where(sub == k, column, 0.0), axis=0, keepdims=True)[:, :1]
        row = row / pivot
        return jnp.where(sub == k, row, full - column * row)

    full = lax.fori_loop(0, 16, eliminate, full)

    def spread(k, carry):
        column = jnp.sum(jnp.where(lane == 16 + k, full, 0.0), axis=1, keepdims=True)
        out_ref[k] = jnp.broadcast_to(column, (16, 128))
        return carry

    lax.fori_loop(0, 16, spread, 0)


def solve_lines(rhs, table_ref, out_ref):
    def forward(i, before):
        value = rhs(i) * table_ref[0, pl.ds(i, 1), :] - table_ref[1, pl.ds(i, 1), :] * before
        out_ref[i] = value
        return value

    last = lax.fori_loop(0, BLK, forward, jnp.zeros((BLK, 128), F32))

    def backward(k, after):
        i = BLK - 2 - k
        value = out_ref[i] - table_ref[1, pl.ds(i, 1), :] * after
        out_ref[i] = value
        return value

    lax.fori_loop(0, BLK - 1, backward, last)


def derivative_rhs(field):
    def rhs(i):
        total = STENCIL[0] * (field[i + 4] - field[i + 2])
        total += STENCIL[1] * (field[i + 5] - field[i + 1])
        return total + STENCIL[2] * (field[i + 6] - field[i])

    return rhs


def filter_rhs(field, slack_ref, first_row):
    def rhs(i):
        total = (field[i] + field[i + 6]) - 6.0 * (field[i + 1] + field[i + 5])
        total += 15.0 * (field[i + 2] + field[i + 4]) - 20.0 * field[i + 3]
        return total * (slack_ref[pl.ds(first_row + i, 1), :] * (1.0 / 64.0))

    return rhs


def kernel(
    u,
    dx,
    dy,
    dz,
    sy,
    sz,
    const_table,
    const_ry,
    const_rz,
    const_profile,
    home,
    uz,
    uy,
    prod,
    gz,
    gy,
    w0,
    wy,
    vy,
    wz,
    vz,
    out,
    es,
    er,
    dxb,
    dtop,
    dbot,
    hm,
    wprof,
    slack_y,
    slack_z,
    all_y,
    all_z,
    tab_y,
    tab_z,
    met_y,
    met_z,
    ry,
    rz,
    zz,
    yz,
    yin,
    yout,
    yback,
    dma,
    loc,
    tin_s,
    tin_r,
    es_s,
    es_r,
    halo_s,
    halo_r,
    zz_s,
    zz_r,
    ya_s,
    ya_r,
    yb_s,
    yb_r,
    tout_s,
    tout_r,
):
    z, x = lax.axis_index("z"), lax.axis_index("x")
    ylo, yhi, core = lax.axis_index("ylo"), lax.axis_index("yhi"), lax.axis_index("core")
    me = (yhi * 2 + ylo) * 2 + core

    def flip(index, bit):
        return 1 - index if bit else index

    def partner(k):
        return {"yhi": flip(yhi, k >> 2), "ylo": flip(ylo, (k >> 1) & 1), "core": flip(core, k & 1)}

    def number(d):
        return (d["yhi"] * 2 + d["ylo"]) * 2 + d["core"]

    def x_lanes(g):
        return pl.ds(pl.multiple_of(g * 128, 128), 128)

    def z_rows(d):
        return pl.multiple_of((d["yhi"] * 2 + d["core"]) * 8, 8)

    def y_rows(d):
        return pl.multiple_of(d["ylo"] * 16, 16)

    here = {"yhi": yhi, "ylo": ylo, "core": core}
    remote = functools.partial(pltpu.make_async_remote_copy, device_id_type=MESH)

    greeted = [partner(k) for k in range(1, 8)]
    greeted += [{"x": lax.rem(x + k, NBZ)} for k in range(1, NBZ)]
    greeted += [{"z": lax.rem(z + k, NBY)} for k in range(1, NBY)]
    barrier = pltpu.get_barrier_semaphore()
    for d in greeted:
        pl.semaphore_signal(barrier, inc=1, device_id=d, device_id_type=MESH)
    pl.semaphore_wait(barrier, len(greeted))

    def exchange_in(c, k):
        d = partner(k)
        return remote(
            src_ref=u.at[c, :, :, x_lanes(number(d))],
            dst_ref=uz.at[c, pl.ds(3 + z_rows(here), 8), pl.ds(y_rows(here), 16), :],
            send_sem=tin_s.at[c, k],
            recv_sem=tin_r.at[c, k],
            device_id=d,
        )

    def keep_in(c):
        return pltpu.make_async_copy(
            u.at[c, :, :, x_lanes(me)],
            uz.at[c, pl.ds(3 + z_rows(here), 8), pl.ds(y_rows(here), 16), :],
            loc.at[c],
        )

    for c in ORDER:
        for k in range(1, 8):
            exchange_in(c, k).start()
        keep_in(c).start()

    first_x = pl.multiple_of(me * 128, 128)
    loads = [
        pltpu.make_async_copy(dx.at[pl.ds(first_x, 128), pl.ds(first_x, 128)], dxb, dma.at[0])
    ]
    for b in range(NBX):
        loads.append(
            pltpu.make_async_copy(dx.at[pl.ds(b * 128, 8), :], dtop.at[b], dma.at[1 + b])
        )
        loads.append(
            pltpu.make_async_copy(dx.at[pl.ds(b * 128 + 120, 8), :], dbot.at[b], dma.at[9 + b])
        )
    for load in loads:
        load.start()
    for load in loads:
        load.wait()

    column_block = iota((8, 1024), 1) // 128
    for b in range(NBX):
        rows = jnp.concatenate([dtop[b, 0:3], dbot[b, 5:8], jnp.zeros((2, 1024), F32)], axis=0)
        hm[pl.ds(b * 8, 8), :] = jnp.where(column_block == b, 0.0, rows)
    for c in range(3):
        product = (u[c] * u[0]).reshape(128, 1024)
        value = lax.dot_general(
            hm[...],
            product,
            (((1,), (1,)), ((), ())),
            precision=HIGHEST,
            preferred_element_type=F32,
        )
        es[:, c] = value.reshape(NBX, 8, 128)

    def exchange_extra(k):
        d = partner(k)
        return remote(
            src_ref=es.at[number(d)],
            dst_ref=er.at[me],
            send_sem=es_s.at[k],
            recv_sem=es_r.at[k],
            device_id=d,
        )

    for k in range(1, 8):
        exchange_extra(k).start()
    er[me] = es[me]

    first_y = pl.multiple_of(z * BLK, BLK)
    first_z = pl.multiple_of(x * BLK, BLK)
    met_y[...] = metric_rows(dy, first_y, 256, pade_off_diagonal(256))
    met_z[...] = metric_rows(dz, first_z, 128, pade_off_diagonal(128))
    slack_y[...] = jnp.broadcast_to(filter_slack(sy, 256), (256, 128))
    half = jnp.broadcast_to(filter_slack(sz, 128), (128, 128))
    slack_z[0:128, :] = half
    slack_z[128:256, :] = half
    block_tables(slack_y, all_y)
    block_tables(slack_z, all_z)

    def pick(i, carry):
        for t in range(4):
            tab_y[t, pl.ds(i, 1), :] = all_y[t, i, pl.ds(z, 1), :]
            tab_z[t, pl.ds(i, 1), :] = all_z[t, i, pl.ds(x, 1), :]
        return carry

    lax.fori_loop(0, BLK, pick, 0)
    invert_reduced(all_y, NBY, ry)
    invert_reduced(all_z, NBZ, rz)

    unit_x = pade_off_diagonal(1024)
    row, col = iota((128, 128), 0), iota((128, 128), 1)
    ends = jnp.where((row == 0) | (row == 127), 1.0 / unit_x, 0.5 / unit_x)
    weight = jnp.where(col == row + 1, ends, jnp.where(col == row - 1, -ends, 0.0))
    metric = lax.dot_general(
        jnp.ones((8, 128), F32),
        dxb[...] * weight,
        (((1,), (1,)), ((), ())),
        precision=HIGHEST,
        preferred_element_type=F32,
    )
    lane, sub = iota((8, 128), 1), iota((8, 128), 0)

    def metric_at(i):
        return jnp.sum(jnp.where(lane == i, metric, 0.0), axis=1, keepdims=True)

    single = (lane < 3) | (lane > 124)
    at_end = jnp.where(sub == 2, metric_at(2), metric_at(125))
    wprof[...] = const_profile[...] * jnp.where(single, 1.0, metric / at_end)

    def halo(stage, c, field, axis, size, side):
        index = {"z": z, "x": x}[axis]
        if side == 0:
            src, dst, to = 32, 0, lax.rem(index + 1, size)
        else:
            src, dst, to = 3, 35, lax.rem(index + size - 1, size)
        return remote(
            src_ref=field.at[c, pl.ds(src, 3)],
            dst_ref=field.at[c, pl.ds(dst, 3)],
            send_sem=halo_s.at[stage, c, side],
            recv_sem=halo_r.at[stage, c, side],
            device_id={axis: to},
        )

    halos = {
        0: functools.partial(halo, 0, field=uz, axis="x", size=NBZ),
        1: functools.partial(halo, 1, field=uy, axis="z", size=NBY),
        2: functools.partial(halo, 2, field=wy, axis="z", size=NBY),
        3: functools.partial(halo, 3, field=wz, axis="x", size=NBZ),
    }

    def start_halo(stage, c):
        for side in range(2):
            halos[stage](c=c, side=side).start()

    def wait_halo(stage, c):
        for side in range(2):
            halos[stage](c=c, side=side).wait_recv()

    def z_ends(op, c, k):
        return remote(
            src_ref=zz.at[op, c, x],
            dst_ref=zz.at[op, c, x],
            send_sem=zz_s.at[op, c, k],
            recv_sem=zz_r.at[op, c, k],
            device_id={"x": lax.rem(x + k, NBZ)},
        )

    def start_z_ends(op, c, solved):
        zz[op, c, x, 0] = solved[c, 0]
        zz[op, c, x, 1] = solved[c, BLK - 1]
        for k in range(1, NBZ):
            z_ends(op, c, k).start()

    def z_neighbours(op, c, inverse):
        for k in range(1, NBZ):
            z_ends(op, c, k).wait_recv()
        values = []
        for target in (8 + lax.rem(x + NBZ - 1, NBZ), lax.rem(x + 1, NBZ)):
            total = None
            for j in range(NBZ):
                for end in range(2):
                    term = inverse[8 * end + j, pl.ds(target, 1), :] * zz[op, c, j, end]
                    total = term if total is None else total + term
            values.append(total)
        return values

    def y_ends(op, c, t):
        return remote(
            src_ref=yz.at[op, c, :, pl.ds(8 * t, 8), :],
            dst_ref=yin.at[op, c, z],
            send_sem=ya_s.at[op, c, t],
            recv_sem=ya_r.at[op, c, z],
            device_id={"z": (4 * c + t) % NBY},
        )

    def start_y_ends(op, c, solved):
        yz[op, c, 0] = solved[c, 0]
        yz[op, c, 1] = solved[c, BLK - 1]
        for t in range(4):
            solver = (4 * c + t) % NBY

            @pl.when(z != solver)
            def _():
                y_ends(op, c, t).start()

            @pl.when(z == solver)
            def _():
                yin[op, c, z] = yz[op, c, :, 8 * t : 8 * t + 8, :]

    def y_answer(op, c, part, i):
        return remote(
            src_ref=yout.at[op, c, i],
            dst_ref=yback.at[op, c, :, pl.ds(pl.multiple_of(part * 8, 8), 8), :],
            send_sem=yb_s.at[op, c, i],
            recv_sem=yb_r.at[op, c, part],
            device_id={"z": i},
        )

    def solve_y_ends(op, c, inverse):
        part = lax.rem(z + NBY - (4 * c) % NBY, NBY)

        @pl.when(part < 4)
        def _():
            for j in range(NBY):

                @pl.when(z != j)
                def _():
                    remote(
                        src_ref=yin.at[op, c, j],
                        dst_ref=yin.at[op, c, j],
                        send_sem=ya_s.at[op, c, 0],
                        recv_sem=ya_r.at[op, c, j],
                        device_id={"z": j},
                    ).wait_recv()

            given = [yin[op, c, j, end] for end in range(2) for j in range(NBY)]

            def ends(i, carry):
                for end, to in ((0, lax.rem(i + NBY - 1, NBY)), (1, lax.rem(i + 1, NBY))):
                    total = None
                    for k in range(16):
                        term = inverse[k, pl.ds(8 * end + i, 1), :] * given[k]
                        total = term if total is None else total + term
                    yout[op, c, to, 1 - end] = total
                return carry

            lax.fori_loop(0, NBY, ends, 0)
            for i in range(NBY):

                @pl.when(z != i)
                def _():
                    y_answer(op, c, part, i).start()

                @pl.when(z == i)
                def _():
                    yback[op, c, :, pl.ds(pl.multiple_of(part * 8, 8), 8), :] = yout[op, c, i]

    def y_neighbours(op, c):
        for t in range(4):

            @pl.when(z != (4 * c + t) % NBY)
            def _():
                remote(
                    src_ref=yout.at[op, c, 0],
                    dst_ref=yback.at[op, c, :, pl.ds(8 * t, 8), :],
                    send_sem=yb_s.at[op, c, 0],
                    recv_sem=yb_r.at[op, c, t],
                    device_id={"z": (4 * c + t) % NBY},
                ).wait_recv()

        return yback[op, c, 0], yback[op, c, 1]

    def lines(i):
        return pl.ds(i, 1)

    for c in ORDER:
        for k in range(1, 8):
            exchange_in(c, k).wait_recv()
        keep_in(c).wait()
        start_halo(0, c)
        flat = uz.at[c].reshape(38 * BLK, 128)

        def turn(i, carry):
            uy[c, 3 + i] = flat[pl.ds(3 * BLK + i, BLK, stride=BLK), :]
            return carry

        lax.fori_loop(0, BLK, turn, 0)
        start_halo(1, c)

    for c in ORDER:
        wait_halo(1, c)

        def multiply(i, carry):
            prod[i] = uy[c, i] * uy[1, i]
            return carry

        lax.fori_loop(0, 38, multiply, 0)
        solve_lines(derivative_rhs(prod), const_table, gy.at[c])
        start_y_ends(0, c, gy)

    for c in ORDER:
        wait_halo(0, c)
    for c in ORDER:

        def multiply(i, carry):
            prod[i] = uz[c, i] * uz[2, i]
            return carry

        lax.fori_loop(0, 38, multiply, 0)
        solve_lines(derivative_rhs(prod), const_table, gz.at[c])
        start_z_ends(0, c, gz)

    for c in ORDER:
        solve_y_ends(0, c, const_ry)

    for k in range(1, 8):
        exchange_extra(k).wait_recv()
    for c in ORDER:

        def along_x(q, carry):
            rows = pl.ds(pl.multiple_of(3 + 8 * q, 1), 8)
            velocity = uz[c, rows]
            product = (velocity * uz[0, rows]).reshape(256, 128)
            inside = lax.dot_general(
                product,
                dxb[...],
                (((1,), (1,)), ((), ())),
                precision=HIGHEST,
                preferred_element_type=F32,
            ).reshape(8, BLK, 128)
            outside = []
            for low in range(2):
                source = ((q // 2) * 2 + low) * 2 + lax.rem(q, 2)
                outside.append(
                    lax.dot_general(
                        er[source, c],
                        wprof[...],
                        (((0,), (0,)), ((), ())),
                        precision=HIGHEST,
                        preferred_element_type=F32,
                    ).reshape(8, 16, 128)
                )
            total = inside + jnp.concatenate(outside, axis=1)
            w0[c, pl.ds(8 * q, 8)] = velocity - 0.1 * total
            return carry

        lax.fori_loop(0, 4, along_x, 0)

    for c in ORDER:
        before, after = z_neighbours(0, c, const_rz)

        def correct_z(i, carry):
            slope = gz[c, i] - const_table[2, lines(i), :] * before
            slope -= const_table[3, lines(i), :] * after
            w0[c, i] = w0[c, i] - (0.1 * met_z[lines(i), :]) * slope
            return carry

        lax.fori_loop(0, BLK, correct_z, 0)
        flat = w0.at[c].reshape(BLK * BLK, 128)
        before, after = y_neighbours(0, c)

        def correct_y(i, carry):
            slope = gy[c, i] - const_table[2, lines(i), :] * before
            slope -= const_table[3, lines(i), :] * after
            wy[c, 3 + i] = flat[pl.ds(i, BLK, stride=BLK), :] - (0.1 * met_y[lines(i), :]) * slope
            return carry

        lax.fori_loop(0, BLK, correct_y, 0)
        start_halo(2, c)

    for c in ORDER:
        wait_halo(2, c)
        solve_lines(filter_rhs(wy.at[c], slack_y, first_y), tab_y, vy.at[c])
        start_y_ends(1, c, vy)
    for c in ORDER:
        solve_y_ends(1, c, ry)
    for c in ORDER:
        before, after = y_neighbours(1, c)

        def smooth_y(i, carry):
            change = vy[c, i] - tab_y[2, lines(i), :] * before
            change -= tab_y[3, lines(i), :] * after
            vy[c, i] = wy[c, 3 + i] + change
            return carry

        lax.fori_loop(0, BLK, smooth_y, 0)
        flat = vy.at[c].reshape(BLK * BLK, 128)

        def turn(i, carry):
            wz[c, 3 + i] = flat[pl.ds(i, BLK, stride=BLK), :]
            return carry

        lax.fori_loop(0, BLK, turn, 0)
        start_halo(3, c)
    for c in ORDER:
        wait_halo(3, c)
        solve_lines(filter_rhs(wz.at[c], slack_z, first_z), tab_z, vz.at[c])
        start_z_ends(1, c, vz)

    def exchange_out(c, k):
        d = partner(k)
        return remote(
            src_ref=out.at[c, pl.ds(z_rows(d), 8), pl.ds(y_rows(d), 16), :],
            dst_ref=home.at[c, :, :, x_lanes(me)],
            send_sem=tout_s.at[c, k],
            recv_sem=tout_r.at[c, k],
            device_id=d,
        )

    def keep_out(c):
        return pltpu.make_async_copy(
            out.at[c, pl.ds(z_rows(here), 8), pl.ds(y_rows(here), 16), :],
            home.at[c, :, :, x_lanes(me)],
            loc.at[3 + c],
        )

    for c in ORDER:
        before, after = z_neighbours(1, c, rz)

        def smooth_z(i, carry):
            change = vz[c, i] - tab_z[2, lines(i), :] * before
            change -= tab_z[3, lines(i), :] * after
            out[c, i] = wz[c, 3 + i] + change
            return carry

        lax.fori_loop(0, BLK, smooth_z, 0)
        for k in range(1, 8):
            exchange_out(c, k).start()
        keep_out(c).start()

    for k in range(1, 8):
        exchange_extra(k).wait_send()
    for c in ORDER:
        for k in range(1, 8):
            exchange_in(c, k).wait_send()
        for stage in range(4):
            for side in range(2):
                halos[stage](c=c, side=side).wait_send()
        for op in range(2):
            for k in range(1, NBZ):
                z_ends(op, c, k).wait_send()
            for t in range(4):

                @pl.when(z != (4 * c + t) % NBY)
                def _():
                    y_ends(op, c, t).wait_send()

            part = lax.rem(z + NBY - (4 * c) % NBY, NBY)

            @pl.when(part < 4)
            def _():
                for i in range(NBY):

                    @pl.when(z != i)
                    def _():
                        y_answer(op, c, part, i).wait_send()

        for k in range(1, 8):
            exchange_out(c, k).wait()
        keep_out(c).wait()


def on_device(velocity, dx, dy, dz, sx, sy, sz):
    table = tridiagonal_tables(SIDE, BLK)
    vmem = pl.BlockSpec(memory_space=pltpu.VMEM)
    big, wide = (3, BLK, BLK, 128), (3, BLK + 6, BLK, 128)
    scratch = [pltpu.VMEM(s, F32) for s in (
        wide, wide, (BLK + 6, BLK, 128), big, big, big, wide, big, wide, big, big,
        (NBX, 3, 8, 128), (NBX, 3, 8, 128), (128, 128), (NBX, 8, 1024), (NBX, 8, 1024), (64, 1024),
        (8, 128), (256, 128), (256, 128), (4, BLK, 8, 128), (4, BLK, 8, 128), (4, BLK, 128),
        (4, BLK, 128), (BLK, 128), (BLK, 128), (16, 16, 128), (16, 16, 128),
        (2, 3, NBZ, 2, BLK, 128), (2, 3, 2, BLK, 128), (2, 3, NBY, 2, 8, 128),
        (2, 3, NBY, 2, 8, 128), (2, 3, 2, BLK, 128),
    )]
    scratch += [pltpu.SemaphoreType.DMA(s) for s in (
        (17,), (6,), (3, 8), (3, 8), (8,), (8,), (4, 3, 2), (4, 3, 2), (2, 3, NBZ), (2, 3, NBZ),
        (2, 3, 4), (2, 3, NBY), (2, 3, NBY), (2, 3, 4), (3, 8), (3, 8),
    )]
    home = pl.pallas_call(
        kernel,
        out_shape=jax.ShapeDtypeStruct(velocity.shape, F32),
        in_specs=[vmem, pl.BlockSpec(memory_space=pl.ANY)] + [vmem] * 8,
        out_specs=vmem,
        scratch_shapes=scratch,
        compiler_params=pltpu.CompilerParams(
            collective_id=1, has_side_effects=True, vmem_limit_bytes=60 * 1024 * 1024
        ),
        name="blocks",
    )(
        velocity, dx, dy, dz, sy, sz,
        jnp.asarray(lanes(table)),
        jnp.asarray(lanes(reduced_inverse(table, NBY).T)),
        jnp.asarray(lanes(reduced_inverse(table, NBZ).T)),
        jnp.asarray(outside_profile(), F32),
    )
    count_c, slab_z, rows_y, width_x = velocity.shape
    result = lax.dot_general(
        home.reshape(-1, width_x), sx, (((1,), (1,)), ((), ())), precision=HIGHEST
    )
    return result.reshape(velocity.shape)


def solution(mesh):
    fine = Mesh(mesh.devices.reshape(SIZES), AXES)
    spec = P(None, ("x", "yhi", "core"), ("z", "ylo"), None)
    return jax.shard_map(
        on_device,
        mesh=fine,
        in_specs=(spec, P(), P(), P(), P(), P(), P()),
        out_specs=spec,
        check_vma=False,
    )
```

time: 312 us -> 103 us (0.33)
  waiting for transfers between devices: 91 us -> 0 us
  Pallas kernels: 0 us -> 90.2 us
  local copies, waits for them, and re-layouts: 85 us -> 4.27 us
  blocking collectives: 75.4 us -> 0 us
  starting transfers between devices: 28.9 us -> 0 us
  matrix products: 30.1 us -> 8.36 us
    all_to_all x4 -> x0, waiting for transfers between devices: 91 us -> none  [the longest x1 32.7 us: pair_to_y(): lax.all_to_all(swap_lines(leading, num_row, rows_y, narrow), 'row', split...]
    pallas_call x0 -> x1, Pallas kernels: none -> 90.2 us  [on_device(): pl.pallas_call(kernel, out_shape=jax.ShapeDtypeStruct(velocity.shape, F32...]
    all_to_all x2 -> x0, blocking collectives: 75.4 us -> none  [the longest x1 45.3 us: single_to_z(): lax.all_to_all(swap_lines(volume, num_row, rows_z, narrow), 'row', split_...]
    reshape x21 -> x0, local copies, waits for them, and re-layouts: 55.1 us -> none  [the longest x6 17.8 us: swap_lines(): return grouped.reshape(inner_count, groups, 3 * local_lines * narrow)]
    all_to_all x4 -> x0, starting transfers between devices: 28.9 us -> none  [the longest x1 8.58 us: on_device(): lax.all_to_all(to_z_lines(tendency), 'col', split_axis=1, concat_axis=0,...]
    dot_general x6 -> x1, matrix products: 30.1 us -> 8.36 us  [on_device(): lax.dot_general(home.reshape(-1, width_x), sx, (((1,), (1,)), ((), ())),...]
    mul x7 -> x0, local copies, waits for them, and re-layouts: 9 us -> none  [the longest x6 7.88 us: times_component(): grouped * grouped[:, :, component:component + 1]]
    another operation x4 -> x3, local copies, waits for them, and re-layouts: 9.29 us -> 4.27 us  [the longest x2 4.97 us: swap_lines(): grouped = volume.reshape(groups, local_lines, 3, inner_count, narrow)]
  transfers between devices with their start and end apart: 4 -> 0, of which waited for: 4 -> 0; matrix products, arithmetic and copies ran while one was open for 8% -> 0% of each run, Pallas kernels for 0% -> 0%
where the time goes in v1:
time: 103 us
  Pallas kernels  90.2 us (88%)
  matrix products  8.36 us (8%)
  local copies, waits for them, and re-layouts  4.27 us (4%)
    pallas_call x1, Pallas kernels, on_device(): pl.pallas_call(kernel, out_shape=jax.ShapeDtypeStruct(velocity.shape, F32...  90.2 us
    dot_general x1, matrix products, on_device(): lax.dot_general(home.reshape(-1, width_x), sx, (((1,), (1,)), ((), ())),...  8.36 us
    another operation x3, local copies, waits for them, and re-layouts  4.27 us

profile of v1, /device:TPU:1, one launch (start us, length us, event | category | flops | bytes accessed | tf_op | source)
XLA Modules:
  0.0 102.9 jit_solution(3576795710667992305)
XLA Ops:
  0.0 1.4 %jit_solution_.9.const_table = f32[4,32,128]{2,1,0:T(8,128)} broadcast(f32[4,32]{1,0:T(4,128)} %constant.8.clone), dimensions={0,1} | broadcast | bytes 66048 | tf_op jit(solution)
  1.4 1.5 %jit_solution_.10.const_ry = f32[16,16,128]{2,1,0:T(8,128)} broadcast(f32[16,16]{1,0:T(8,128)} %constant.9.clone), dimensions={0,1} | broadcast | bytes 132096 | tf_op jit(solution)
  2.8 1.4 %jit_solution_.11.const_rz = f32[16,16,128]{2,1,0:T(8,128)} broadcast(f32[16,16]{1,0:T(8,128)} %constant.10.clone), dimensions={0,1} | broadcast | bytes 132096 | tf_op jit(solution)
  4.3 90.2 %blocks.1 = f32[3,8,16,1024]{3,2,1,0:T(8,128)} custom-call(f32[3,8,16,1024]{3,2,1,0:T(8,128)} %u.1, f32[1024,1024]{1,0:T(8,128)} %dx.1, f32[256,256]{1,0:T(8,128)} %dy.1, f32[128,128]{1,0:T(8,128)} %dz.1, f32[256,256]{1,0:T(8,128)} %sy.1, f32[128,128]{1,0:T(8,128)} %sz.1, f32[4,32,128]{2,1,0:T(8,128)} %jit_solution_.9.const_table, ...), custom_call_target="tpu_custom_call" | custom-call | tf_op jit(solution)/shard_map/blocks/pallas_call | solution.py:764
  94.5 8.4 %fusion = f32[3,8,16,1024]{3,2,1,0:T(8,128)} fusion(f32[3,8,16,1024]{3,2,1,0:T(8,128)} %blocks.1, f32[1024,1024]{1,0:T(8,128)} %param.15), kind=kOutput, calls=%fused_computation | convolution fusion | flops 4831838208 | bytes 7340032 | tf_op jit(solution)/shard_map/dot_general | solution.py:782

commit v2 on v1

v2 whole, which is shorter than its diff:
```python
import functools

import jax
import jax.numpy as jnp
import numpy as np
from jax import lax
from jax.experimental import pallas as pl
from jax.experimental.pallas import tpu as pltpu
from jax.sharding import Mesh
from jax.sharding import PartitionSpec as P

AXES = ("z", "ylo", "x", "yhi", "core")
SIZES = (8, 2, 4, 2, 2)
MESH = pl.DeviceIdType.MESH
HIGHEST = lax.Precision.HIGHEST
F32 = jnp.float32
BLK = 32
NBY, NBZ, NBX = 8, 4, 8
ORDER = (1, 2, 0)
SIDE = 9.0 / 20.0
STENCIL = (63.0 / 80.0, 9.0 / 100.0, -7.0 / 1200.0)


def tridiagonal_tables(side, count):
    piv, cp = np.zeros(count), np.zeros(count)
    before = 0.0
    for i in range(count):
        piv[i] = 1.0 / (1.0 - side * before)
        before = cp[i] = side * piv[i]
    first, last = np.zeros(count), np.zeros(count)
    first[0] = cp[0]
    for i in range(1, count):
        first[i] = -cp[i] * first[i - 1]
    last[-1] = cp[-1]
    for i in range(count - 2, -1, -1):
        first[i] -= cp[i] * first[i + 1]
        last[i] = -cp[i] * last[i + 1]
    return np.stack([piv, cp, first, last])


def reduced_inverse(table, blocks):
    first, last = table[2], table[3]
    full = np.eye(16)
    for i in range(blocks):
        before, after = 8 + (i - 1) % blocks, (i + 1) % blocks
        full[i, before] += first[0]
        full[i, after] += last[0]
        full[8 + i, before] += first[-1]
        full[8 + i, after] += last[-1]
    return np.linalg.inv(full)


def pade_off_diagonal(count):
    left = np.eye(count) + SIDE * (np.roll(np.eye(count), 1, 1) + np.roll(np.eye(count), -1, 1))
    right = sum(
        w * (np.roll(np.eye(count), k + 1, 1) - np.roll(np.eye(count), -k - 1, 1))
        for k, w in enumerate(STENCIL)
    )
    return float(np.linalg.solve(left, right)[0, 1])


def outside_profile():
    inner = 122
    matrix = np.eye(inner) + SIDE * (np.eye(inner, k=1) + np.eye(inner, k=-1))
    profile = np.zeros((8, 128))
    for e, row in enumerate((0, 1, 2, 125, 126, 127)):
        profile[e, row] = 1.0
    unit = np.zeros(inner)
    unit[0] = -SIDE
    profile[2, 3:125] = np.linalg.solve(matrix, unit)
    profile[3, 3:125] = np.linalg.solve(matrix, unit[::-1])
    return profile


def iota(shape, dim):
    return lax.broadcasted_iota(jnp.int32, shape, dim)


def wrapped_offset(shape, first_row, count):
    offset = iota(shape, 1) - iota(shape, 0) - first_row
    return jnp.where(offset < 0, offset + count, offset)


def metric_rows(matrix_ref, first_row, count, unit):
    block = matrix_ref[pl.ds(first_row, BLK), :]
    offset = wrapped_offset(block.shape, first_row, count)
    weight = jnp.where(offset == 1, 0.5 / unit, jnp.where(offset == count - 1, -0.5 / unit, 0.0))
    return jnp.broadcast_to(jnp.sum(block * weight, axis=1, keepdims=True), (BLK, 128))


def filter_slack(matrix_ref, count):
    shape = (count, count)
    offset = wrapped_offset(shape, 0, count)
    change = matrix_ref[...] - jnp.where(offset == 0, 1.0, 0.0)
    around = 0.5 * (pltpu.roll(change, 1, 0) + pltpu.roll(change, count - 1, 0))
    sixth = jnp.zeros(shape, F32)
    for k, w in enumerate((-20.0, 15.0, -6.0, 1.0)):
        sixth = jnp.where((offset == k) | (offset == (count - k) % count), w / 64.0, sixth)
    basis = sixth + around
    top = jnp.sum((change + around) * basis, axis=1, keepdims=True)
    return top / jnp.sum(basis * basis, axis=1, keepdims=True)


def block_tables(slack_ref, all_ref):
    def side(i):
        return 0.5 - 0.5 * slack_ref[pl.ds(i, 8, stride=BLK), :]

    def forward(i, carry):
        before, first = carry
        a = side(i)
        piv = 1.0 / (1.0 - a * before)
        cp = a * piv
        first = jnp.where(i == 0, cp, -cp * first)
        all_ref[0, i] = piv
        all_ref[1, i] = cp
        all_ref[2, i] = first
        return cp, first

    zero = jnp.zeros((8, 128), F32)
    lax.fori_loop(0, BLK, forward, (zero, zero))

    def backward(k, carry):
        first, last = carry
        i = BLK - 1 - k
        cp = all_ref[1, i]
        first = all_ref[2, i] - cp * first
        last = jnp.where(k == 0, cp, -cp * last)
        all_ref[2, i] = first
        all_ref[3, i] = last
        return first, last

    lax.fori_loop(0, BLK, backward, (zero, zero))


def invert_reduced(all_ref, blocks):
    sub, lane = iota((8, 128), 0), iota((8, 128), 1)
    before = 8 + jnp.where(sub == 0, blocks - 1, sub - 1)
    after = jnp.where(sub == blocks - 1, 0, sub + 1)
    valid = sub < blocks

    def rows(own, first, last):
        value = jnp.where(lane == own, 1.0, 0.0)
        value += jnp.where(valid & (lane == before), first, 0.0)
        return value + jnp.where(valid & (lane == after), last, 0.0)

    full = jnp.concatenate(
        [
            rows(sub, all_ref[2, 0], all_ref[3, 0]),
            rows(8 + sub, all_ref[2, BLK - 1], all_ref[3, BLK - 1]),
        ],
        axis=0,
    )
    sub, lane = iota((16, 128), 0), iota((16, 128), 1)
    full += jnp.where(lane == 16 + sub, 1.0, 0.0)

    def eliminate(k, full):
        column = jnp.sum(jnp.where(lane == k, full, 0.0), axis=1, keepdims=True)
        row = jnp.sum(jnp.where(sub == k, full, 0.0), axis=0, keepdims=True)
        pivot = jnp.sum(jnp.where(sub == k, column, 0.0), axis=0, keepdims=True)[:, :1]
        row = row / pivot
        return jnp.where(sub == k, row, full - column * row)

    return lax.fori_loop(0, 16, eliminate, full)


def loop(count, body, carry, unroll=8):
    steps = count // unroll

    def several(k, carry):
        for j in range(unroll):
            carry = body(k * unroll + j, carry)
        return carry

    carry = lax.fori_loop(0, steps, several, carry)
    for i in range(steps * unroll, count):
        carry = body(i, carry)
    return carry


def each(count, body, unroll=8):
    def step(i, carry):
        body(i)
        return carry

    loop(count, step, 0, unroll)


def halves(value):
    high = value.astype(jnp.bfloat16)
    return high, (value - high.astype(F32)).astype(jnp.bfloat16)


def contract(a, b, dims):
    return lax.dot_general(a, b, (dims, ((), ())), preferred_element_type=F32)


def solve_lines(rhs, table_ref, out_ref):
    def forward(i, before):
        value = rhs(i) * table_ref[0, pl.ds(i, 1), :] - table_ref[1, pl.ds(i, 1), :] * before
        out_ref[i] = value
        return value

    last = loop(BLK, forward, jnp.zeros((BLK, 128), F32))

    def backward(k, after):
        i = BLK - 2 - k
        value = out_ref[i] - table_ref[1, pl.ds(i, 1), :] * after
        out_ref[i] = value
        return value

    loop(BLK - 1, backward, last)


def derivative_rhs(field):
    def rhs(i):
        total = STENCIL[0] * (field[i + 4] - field[i + 2])
        total += STENCIL[1] * (field[i + 5] - field[i + 1])
        return total + STENCIL[2] * (field[i + 6] - field[i])

    return rhs


def filter_rhs(field, slack_ref, first_row):
    def rhs(i):
        total = (field[i] + field[i + 6]) - 6.0 * (field[i + 1] + field[i + 5])
        total += 15.0 * (field[i + 2] + field[i + 4]) - 20.0 * field[i + 3]
        return total * (slack_ref[pl.ds(first_row + i, 1), :] * (1.0 / 64.0))

    return rhs


def kernel(
    u_hbm,
    dx,
    dy_hbm,
    dz_hbm,
    sy_hbm,
    sz_hbm,
    const_hbm,
    home,
    u,
    dy,
    dz,
    sy,
    sz,
    const,
    uz,
    uy,
    prod,
    gz,
    gy,
    w0,
    wz,
    vz,
    qy,
    vy,
    turned,
    out,
    edge,
    fix,
    es,
    er,
    dxb,
    dtop,
    dbot,
    inner,
    outer,
    slack_y,
    slack_z,
    all_y,
    all_z,
    tab_d,
    tab_y,
    tab_z,
    met_y,
    met_z,
    rdy,
    rdz,
    rsy,
    rsz,
    ze,
    ye,
    dma,
    loc,
    tin_s,
    tin_r,
    es_s,
    es_r,
    halo_s,
    halo_r,
    ze_s,
    ze_r,
    ye_s,
    ye_r,
    tout_s,
    tout_r,
    edge_s,
    edge_r,
):
    z, x = lax.axis_index("z"), lax.axis_index("x")
    ylo, yhi, core = lax.axis_index("ylo"), lax.axis_index("yhi"), lax.axis_index("core")
    me = (yhi * 2 + ylo) * 2 + core
    first_y = pl.multiple_of(z * BLK, BLK)
    first_z = pl.multiple_of(x * BLK, BLK)
    started = []

    def flip(index, bit):
        return 1 - index if bit else index

    def partner(k):
        return {"yhi": flip(yhi, k >> 2), "ylo": flip(ylo, (k >> 1) & 1), "core": flip(core, k & 1)}

    def number(d):
        return (d["yhi"] * 2 + d["ylo"]) * 2 + d["core"]

    def x_lanes(g):
        return pl.ds(pl.multiple_of(g * 128, 128), 128)

    def z_rows(d):
        return pl.multiple_of((d["yhi"] * 2 + d["core"]) * 8, 8)

    def y_rows(d):
        return pl.multiple_of(d["ylo"] * 16, 16)

    def lines(i):
        return pl.ds(i, 1)

    here = {"yhi": yhi, "ylo": ylo, "core": core}
    remote = functools.partial(pltpu.make_async_remote_copy, device_id_type=MESH)

    def start(copy):
        copy.start()
        started.append(copy)

    greeted = [partner(k) for k in range(1, 8)]
    greeted += [{"x": lax.rem(x + k, NBZ)} for k in range(1, NBZ)]
    greeted += [{"z": lax.rem(z + k, NBY)} for k in range(1, NBY)]
    barrier = pltpu.get_barrier_semaphore()
    for d in greeted:
        pl.semaphore_signal(barrier, inc=1, device_id=d, device_id_type=MESH)

    first_x = pl.multiple_of(me * 128, 128)
    loads = [
        pltpu.make_async_copy(dx.at[pl.ds(first_x, 128), pl.ds(first_x, 128)], dxb, dma.at[0])
    ]
    for b in range(NBX):
        loads.append(
            pltpu.make_async_copy(dx.at[pl.ds(b * 128, 8), :], dtop.at[b], dma.at[1 + b])
        )
        loads.append(
            pltpu.make_async_copy(dx.at[pl.ds(b * 128 + 120, 8), :], dbot.at[b], dma.at[9 + b])
        )
    pairs = ((u_hbm, u), (const_hbm, const), (dy_hbm, dy), (dz_hbm, dz), (sy_hbm, sy), (sz_hbm, sz))
    for i, (src, dst) in enumerate(pairs):
        loads.append(pltpu.make_async_copy(src, dst, dma.at[17 + i]))
    for load in loads:
        load.start()

    pl.semaphore_wait(barrier, len(greeted))

    def exchange_in(c, k):
        d = partner(k)
        return remote(
            src_ref=u_hbm.at[c, :, :, x_lanes(number(d))],
            dst_ref=uz.at[c, pl.ds(3 + z_rows(here), 8), pl.ds(y_rows(here), 16), :],
            send_sem=tin_s.at[c, k],
            recv_sem=tin_r.at[c, k],
            device_id=d,
        )

    def keep_in(c):
        return pltpu.make_async_copy(
            u_hbm.at[c, :, :, x_lanes(me)],
            uz.at[c, pl.ds(3 + z_rows(here), 8), pl.ds(y_rows(here), 16), :],
            loc.at[c],
        )

    def begin():
        for c in ORDER:
            for k in range(1, 8):
                start(exchange_in(c, k))
            keep_in(c).start()

    def exchange_extra(k):
        d = partner(k)
        return remote(
            src_ref=es.at[number(d)],
            dst_ref=er.at[me],
            send_sem=es_s.at[k],
            recv_sem=es_r.at[k],
            device_id=d,
        )

    def extras():
        for load in loads:
            load.wait()
        column_block = iota((8, 1024), 1) // 128
        picked = []
        for b in range(NBX):
            rows = jnp.concatenate([dtop[b, 0:3], dbot[b, 5:8], jnp.zeros((2, 1024), F32)], axis=0)
            picked.append(jnp.where(column_block == b, 0.0, rows))
        high, low = halves(jnp.concatenate(picked, axis=0))
        both = jnp.concatenate([high, low], axis=0)
        for c in range(3):
            p_high, p_low = halves((u[c] * u[0]).reshape(128, 1024))
            value = contract(both, p_high, ((1,), (1,)))
            value = value[:64] + value[64:] + contract(high, p_low, ((1,), (1,)))
            es[:, c] = value.reshape(NBX, 8, 128)
        for k in range(1, 8):
            start(exchange_extra(k))
        er[me] = es[me]

    def spread(full, first, out_ref):
        lane = iota(full.shape, 1)

        def one(k):
            column = jnp.sum(jnp.where(lane == first + k, full, 0.0), axis=1, keepdims=True)
            out_ref[k] = jnp.broadcast_to(column, full.shape)

        each(out_ref.shape[0], one, 4)

    def derivative_tables():
        spread(const[0:16, :], 0, rdy)
        spread(const[16:32, :], 0, rdz)
        spread(const[32:64, :], 0, tab_d)
        met_y[...] = metric_rows(dy, first_y, 256, pade_off_diagonal(256)) * 0.1
        met_z[...] = metric_rows(dz, first_z, 128, pade_off_diagonal(128)) * 0.1

    def x_tables():
        unit_x = pade_off_diagonal(1024)
        row, col = iota((128, 128), 0), iota((128, 128), 1)
        ends = jnp.where((row == 0) | (row == 127), 1.0 / unit_x, 0.5 / unit_x)
        weight = jnp.where(col == row + 1, ends, jnp.where(col == row - 1, -ends, 0.0))
        metric = lax.dot_general(
            jnp.ones((8, 128), F32),
            dxb[...] * weight,
            (((1,), (1,)), ((), ())),
            precision=HIGHEST,
            preferred_element_type=F32,
        )
        lane, sub = iota((8, 128), 1), iota((8, 128), 0)

        def metric_at(i):
            return jnp.sum(jnp.where(lane == i, metric, 0.0), axis=1, keepdims=True)

        single = (lane < 3) | (lane > 124)
        at_end = jnp.where(sub == 2, metric_at(2), metric_at(125))
        profile = const[64:72, :] * jnp.where(single, 1.0, metric / at_end)
        high, low = halves(profile)
        outer[...] = jnp.concatenate([high, high, low, jnp.zeros_like(low)], axis=0)
        high, low = halves(dxb[...].T)
        inner[0:128, 0:128] = high
        inner[128:256, 0:128] = high
        inner[0:128, 128:256] = low
        inner[128:256, 128:256] = jnp.zeros_like(low)

    def filter_tables():
        slack_y[...] = jnp.broadcast_to(filter_slack(sy, 256), (256, 128))
        half = jnp.broadcast_to(filter_slack(sz, 128), (128, 128))
        slack_z[0:128, :] = half
        slack_z[128:256, :] = half
        block_tables(slack_y, all_y)
        block_tables(slack_z, all_z)

        def pick(i):
            for t in range(4):
                tab_y[t, lines(i), :] = all_y[t, i, pl.ds(z, 1), :]
                tab_z[t, lines(i), :] = all_z[t, i, pl.ds(x, 1), :]

        each(BLK, pick, 4)
        spread(invert_reduced(all_y, NBY), 16, rsy)
        spread(invert_reduced(all_z, NBZ), 16, rsz)

    def halo(stage, c, side):
        field, axis, size = ((uz, "x", NBZ), (uy, "z", NBY), (wz, "x", NBZ), (qy, "z", NBY))[stage]
        index = {"z": z, "x": x}[axis]
        if side == 0:
            src, dst, to = 32, 0, lax.rem(index + 1, size)
        else:
            src, dst, to = 3, 35, lax.rem(index + size - 1, size)
        return remote(
            src_ref=field.at[c, pl.ds(src, 3)],
            dst_ref=field.at[c, pl.ds(dst, 3)],
            send_sem=halo_s.at[stage, c, side],
            recv_sem=halo_r.at[stage, c, side],
            device_id={axis: to},
        )

    def start_halo(stage, c):
        for side in range(2):
            start(halo(stage, c, side))

    def wait_halo(stage, c):
        for side in range(2):
            halo(stage, c, side).wait_recv()

    def end_copy(axis, op, c, k):
        buf, send, recv = {"x": (ze, ze_s, ze_r), "z": (ye, ye_s, ye_r)}[axis]
        index, size = {"x": (x, NBZ), "z": (z, NBY)}[axis]
        return remote(
            src_ref=buf.at[op, c, index],
            dst_ref=buf.at[op, c, index],
            send_sem=send.at[op, c, k],
            recv_sem=recv.at[op, c, k],
            device_id={axis: lax.rem(index + k, size)},
        )

    def start_ends(axis, op, c, solved):
        buf, index, size = {"x": (ze, x, NBZ), "z": (ye, z, NBY)}[axis]
        buf[op, c, index, 0] = solved[c, 0]
        buf[op, c, index, 1] = solved[c, BLK - 1]
        for k in sorted(range(1, size), key=lambda k: -min(k, size - k)):
            start(end_copy(axis, op, c, k))

    def neighbours(axis, op, c, inverse):
        buf, index, size = {"x": (ze, x, NBZ), "z": (ye, z, NBY)}[axis]
        for k in range(1, size):
            end_copy(axis, op, c, k).wait_recv()
        values = []
        for target in (8 + lax.rem(index + size - 1, size), lax.rem(index + 1, size)):
            total = None
            for j in range(size):
                for end in range(2):
                    term = inverse[8 * end + j, lines(target), :] * buf[op, c, j, end]
                    total = term if total is None else total + term
            values.append(total)
        return values

    def turn(src, dst, first):
        flat = src.reshape(src.shape[0] * BLK, 128)

        def one(i):
            dst[first[1] + i] = flat[pl.ds(first[0] * BLK + i, BLK, stride=BLK), :]

        each(BLK, one)

    def minus_ends(value, table, i, before, after):
        return value - table[2, lines(i), :] * before - table[3, lines(i), :] * after

    def arrive(c):
        for k in range(1, 8):
            exchange_in(c, k).wait_recv()
        keep_in(c).wait()
        start_halo(0, c)
        turn(uz.at[c], uy.at[c], (3, 3))
        start_halo(1, c)

    def slope_y(c):
        wait_halo(1, c)

        def multiply(i):
            prod[i] = uy[c, i] * uy[1, i]

        each(38, multiply)
        solve_lines(derivative_rhs(prod), tab_d, gy.at[c])
        start_ends("z", 0, c, gy)

    def slope_z(c):
        wait_halo(0, c)

        def multiply(i):
            prod[i] = uz[c, i] * uz[2, i]

        each(38, multiply)
        solve_lines(derivative_rhs(prod), tab_d, gz.at[c])
        start_ends("x", 0, c, gz)

    def slope_x(c):
        if c == ORDER[0]:
            for k in range(1, 8):
                exchange_extra(k).wait_recv()

        def part(q, carry):
            rows = pl.ds(3 + 8 * q, 8)
            velocity = uz[c, rows]
            high, low = halves((velocity * uz[0, rows]).reshape(256, 128))
            value = contract(jnp.concatenate([high, low], axis=1), inner[...], ((1,), (0,)))
            total = (value[:, :128] + value[:, 128:]).reshape(8, BLK, 128)
            outside = []
            for low_y in range(2):
                source = ((q // 2) * 2 + low_y) * 2 + lax.rem(q, 2)
                high, low = halves(er[source, c])
                given = jnp.concatenate([high, low, high, jnp.zeros_like(low)], axis=0)
                value = contract(given, outer[...], ((0,), (0,)))
                outside.append(value.reshape(8, 16, 128))
            total += jnp.concatenate(outside, axis=1)
            w0[c, pl.ds(8 * q, 8)] = velocity - 0.1 * total
            return carry

        lax.fori_loop(0, 4, part, 0)

    def advance(c):
        before, after = neighbours("z", 0, c, rdy)

        def correct_y(i):
            gy[c, i] = met_y[lines(i), :] * minus_ends(gy[c, i], tab_d, i, before, after)

        each(BLK, correct_y)
        turn(gy.at[c], turned, (0, 0))
        before_z, after_z = neighbours("x", 0, c, rdz)

        def correct_z(i):
            slope = met_z[lines(i), :] * minus_ends(gz[c, i], tab_d, i, before_z, after_z)
            wz[c, 3 + i] = w0[c, i] - slope - turned[i]

        each(BLK, correct_z)
        start_halo(2, c)

    def smooth_z(c):
        wait_halo(2, c)
        solve_lines(filter_rhs(wz.at[c], slack_z, first_z), tab_z, vz.at[c])
        start_ends("x", 1, c, vz)

    def smoothed_z(c):
        before, after = neighbours("x", 1, c, rsz)

        def one(i):
            turned[i] = wz[c, 3 + i] + minus_ends(vz[c, i], tab_z, i, before, after)

        each(BLK, one)
        turn(turned, qy.at[c], (0, 3))
        start_halo(3, c)

    def exchange_out(c, k):
        d = partner(k)
        return remote(
            src_ref=out.at[c, pl.ds(z_rows(d), 8), pl.ds(y_rows(d), 16), :],
            dst_ref=home.at[c, :, :, x_lanes(me)],
            send_sem=tout_s.at[c, k],
            recv_sem=tout_r.at[c, k],
            device_id=d,
        )

    def keep_out(c):
        return pltpu.make_async_copy(
            out.at[c, pl.ds(z_rows(here), 8), pl.ds(y_rows(here), 16), :],
            home.at[c, :, :, x_lanes(me)],
            loc.at[3 + c],
        )

    def smooth_y(c):
        wait_halo(3, c)
        solve_lines(filter_rhs(qy.at[c], slack_y, first_y), tab_y, vy.at[c])
        start_ends("z", 1, c, vy)

        def one(i):
            turned[i] = qy[c, 3 + i] + vy[c, i]

        each(BLK, one)
        turn(turned, out.at[c], (0, 0))
        for k in (4, 5, 2, 6, 3, 7, 1):
            start(exchange_out(c, k))
        keep_out(c).start()

    def edge_copy(c, k):
        d = partner(k)
        return remote(
            src_ref=edge.at[c, :, pl.ds(z_rows(d), 8), :],
            dst_ref=fix.at[c, :, :, x_lanes(me)],
            send_sem=edge_s.at[c, k],
            recv_sem=edge_r.at[c, k],
            device_id=d,
        )

    def correct(c):
        before, after = neighbours("z", 1, c, rsy)
        edge[c, 0] = before
        edge[c, 1] = after
        for k in (4, 5, 2, 6, 3, 7, 1):
            start(edge_copy(c, k))
        fix[c, :, :, x_lanes(me)] = edge[c, :, pl.ds(z_rows(here), 8), :]

    def leave(c):
        for k in range(1, 8):
            exchange_out(c, k).wait_recv()
        keep_out(c).wait()
        for k in range(1, 8):
            edge_copy(c, k).wait_recv()
        first = tab_y[2, pl.ds(y_rows(here), 16), :]
        last = tab_y[3, pl.ds(y_rows(here), 16), :]

        def one(g):
            lanes = x_lanes(g)
            before, after = fix[c, 0, :, lanes], fix[c, 1, :, lanes]
            for i in range(8):
                value = home[c, i, :, lanes] - first * before[i : i + 1]
                home[c, i, :, lanes] = value - last * after[i : i + 1]

        each(8, one, 2)

    one, two, three = ORDER
    steps = [
        (begin,),
        (extras,),
        (derivative_tables,),
        (arrive, one),
        (x_tables,),
        (slope_y, one),
        (filter_tables,),
        (arrive, two),
        (slope_y, two),
        (slope_z, two),
        (slope_z, one),
        (arrive, three),
        (slope_x, one),
        (advance, one),
        (slope_y, three),
        (slope_z, three),
        (slope_x, two),
        (advance, two),
        (smooth_z, one),
        (slope_x, three),
        (smooth_z, two),
        (advance, three),
        (smoothed_z, one),
        (smoothed_z, two),
        (smooth_z, three),
        (smooth_y, one),
        (smooth_y, two),
        (smoothed_z, three),
        (correct, one),
        (correct, two),
        (smooth_y, three),
        (leave, one),
        (leave, two),
        (correct, three),
        (leave, three),
    ]
    for step in steps[:STOP]:
        step[0](*step[1:])
    for copy in started:
        copy.wait_send()


STOP = 99


def on_device(velocity, dx, dy, dz, sx, sy, sz):
    table = tridiagonal_tables(SIDE, BLK)
    const = np.zeros((72, 128), np.float32)
    const[0:16, :16] = reduced_inverse(table, NBY)
    const[16:32, :16] = reduced_inverse(table, NBZ)
    const[32:64, :4] = table.T
    const[64:72] = outside_profile()
    vmem = pl.BlockSpec(memory_space=pltpu.VMEM)
    big, wide, one = (3, BLK, BLK, 128), (3, BLK + 6, BLK, 128), (BLK, BLK, 128)
    shapes = (
        velocity.shape, (256, 256), (128, 128), (256, 256), (128, 128), (72, 128),
        wide, wide, (BLK + 6, BLK, 128), big, big, big, wide, big, wide, big, one, big,
        (3, 2, BLK, 128), (3, 2, 8, 1024),
        (NBX, 3, 8, 128), (NBX, 3, 8, 128), (128, 128), (NBX, 8, 1024), (NBX, 8, 1024),
    )
    scratch = [pltpu.VMEM(s, F32) for s in shapes]
    scratch += [pltpu.VMEM((256, 256), jnp.bfloat16), pltpu.VMEM((32, 128), jnp.bfloat16)]
    shapes = (
        (256, 128), (256, 128), (4, BLK, 8, 128), (4, BLK, 8, 128),
        (4, BLK, 128), (4, BLK, 128), (4, BLK, 128), (BLK, 128), (BLK, 128),
        (16, 16, 128), (16, 16, 128), (16, 16, 128), (16, 16, 128),
        (2, 3, NBZ, 2, BLK, 128), (2, 3, NBY, 2, BLK, 128),
    )
    scratch += [pltpu.VMEM(s, F32) for s in shapes]
    counts = (
        (23,), (6,), (3, 8), (3, 8), (8,), (8,), (4, 3, 2), (4, 3, 2),
        (2, 3, NBZ), (2, 3, NBZ), (2, 3, NBY), (2, 3, NBY), (3, 8), (3, 8),
        (3, 8), (3, 8),
    )
    scratch += [pltpu.SemaphoreType.DMA(s) for s in counts]
    home = pl.pallas_call(
        kernel,
        out_shape=jax.ShapeDtypeStruct(velocity.shape, F32),
        in_specs=[pl.BlockSpec(memory_space=pl.ANY)] * 7,
        out_specs=vmem,
        scratch_shapes=scratch,
        compiler_params=pltpu.CompilerParams(
            collective_id=1, has_side_effects=True, vmem_limit_bytes=60 * 1024 * 1024
        ),
        name="blocks",
    )(velocity, dx, dy, dz, sy, sz, jnp.asarray(const))
    width_x = velocity.shape[3]
    result = lax.dot_general(
        home.reshape(-1, width_x), sx, (((1,), (1,)), ((), ())), precision=lax.Precision.HIGH
    )
    return result.reshape(velocity.shape)


def solution(mesh):
    fine = Mesh(mesh.devices.reshape(SIZES), AXES)
    spec = P(None, ("x", "yhi", "core"), ("z", "ylo"), None)
    return jax.shard_map(
        on_device,
        mesh=fine,
        in_specs=(spec, P(), P(), P(), P(), P(), P()),
        out_specs=spec,
        check_vma=False,
    )
```

time: 103 us -> 90.9 us (0.88)
  Pallas kernels: 90.2 us -> 84.3 us
  local copies, waits for them, and re-layouts: 4.27 us -> 0 us
  matrix products: 8.36 us -> 6.49 us
    pallas_call x1, Pallas kernels: 90.2 us -> 84.3 us  [on_device(): pl.pallas_call(kernel, out_shape=jax.ShapeDtypeStruct(velocity.shape, F32...]
    another operation x3 -> x0, local copies, waits for them, and re-layouts: 4.27 us -> none
    dot_general x1, matrix products: 8.36 us -> 6.49 us  [on_device(): lax.dot_general(home.reshape(-1, width_x), sx, (((1,), (1,)), ((), ())),...]
where the time goes in v2:
time: 90.9 us; the launch traced here: 90.8 us
  Pallas kernels  84.3 us (93%)
  matrix products  6.49 us (7%)
    pallas_call x1, Pallas kernels, on_device(): pl.pallas_call(kernel, out_shape=jax.ShapeDtypeStruct(velocity.shape, F32...  84.3 us
    dot_general x1, matrix products, on_device(): lax.dot_general(home.reshape(-1, width_x), sx, (((1,), (1,)), ((), ())),...  6.49 us

profile of v2, /device:TPU:1, one launch (start us, length us, event | category | flops | bytes accessed | tf_op | source)
XLA Modules:
  0.0 90.8 jit_solution(18007771451464243561)
XLA Ops:
  0.0 84.3 %blocks.1 = f32[3,8,16,1024]{3,2,1,0:T(8,128)} custom-call(f32[3,8,16,1024]{3,2,1,0:T(8,128)} %u_hbm.1, f32[1024,1024]{1,0:T(8,128)} %dx.1, f32[256,256]{1,0:T(8,128)} %dy_hbm.1, f32[128,128]{1,0:T(8,128)} %dz_hbm.1, f32[256,256]{1,0:T(8,128)} %sy_hbm.1, f32[128,128]{1,0:T(8,128)} %sz_hbm.1, f32[72,128]{1,0:T(8,128)} %constant.2.clone.const_hbm), custom_call_target="tpu_custom_call" | custom-call | tf_op jit(solution)/shard_map/blocks/pallas_call | solution.py:768
  84.3 6.5 %fusion = f32[3,8,16,1024]{3,2,1,0:T(8,128)} fusion(f32[3,8,16,1024]{3,2,1,0:T(8,128)} %blocks.1, f32[1024,1024]{1,0:T(8,128)} %param.12), kind=kOutput, calls=%fused_computation | convolution fusion | flops 2415919104 | bytes 7340032 | tf_op jit(solution)/shard_map/dot_general | solution.py:780

commit v3 on v2

--- a/solution.py
+++ b/solution.py
@@ -375,11 +375,20 @@
             loc.at[c],
         )
 
+    far_first = (4, 5, 2, 6, 3, 7, 1)
+
     def begin():
-        for c in ORDER:
-            for k in range(1, 8):
-                start(exchange_in(c, k))
+        for c in ORDER[:2]:
+            for k in far_first:
+                exchange_in(c, k).start()
             keep_in(c).start()
+
+    def begin_last():
+        keep_in(ORDER[2]).start()
+        for k in far_first:
+            for c in ORDER[:2]:
+                exchange_in(c, k).wait_send()
+            start(exchange_in(ORDER[2], k))
 
     def exchange_extra(k):
         d = partner(k)
@@ -648,7 +657,7 @@
 
         each(BLK, one)
         turn(turned, out.at[c], (0, 0))
-        for k in (4, 5, 2, 6, 3, 7, 1):
+        for k in far_first:
             start(exchange_out(c, k))
         keep_out(c).start()
 
@@ -666,7 +675,7 @@
         before, after = neighbours("z", 1, c, rsy)
         edge[c, 0] = before
         edge[c, 1] = after
-        for k in (4, 5, 2, 6, 3, 7, 1):
+        for k in far_first:
             start(edge_copy(c, k))
         fix[c, :, :, x_lanes(me)] = edge[c, :, pl.ds(z_rows(here), 8), :]
 
@@ -693,11 +702,12 @@
         (begin,),
         (extras,),
         (derivative_tables,),
+        (x_tables,),
+        (filter_tables,),
+        (begin_last,),
         (arrive, one),
-        (x_tables,),
+        (arrive, two),
         (slope_y, one),
-        (filter_tables,),
-        (arrive, two),
         (slope_y, two),
         (slope_z, two),
         (slope_z, one),
@@ -711,19 +721,19 @@
         (smooth_z, one),
         (slope_x, three),
         (smooth_z, two),
+        (smoothed_z, one),
         (advance, three),
-        (smoothed_z, one),
         (smoothed_z, two),
+        (smooth_y, one),
         (smooth_z, three),
-        (smooth_y, one),
         (smooth_y, two),
         (smoothed_z, three),
         (correct, one),
+        (smooth_y, three),
         (correct, two),
-        (smooth_y, three),
         (leave, one),
+        (correct, three),
         (leave, two),
-        (correct, three),
         (leave, three),
     ]
     for step in steps[:STOP]:

time: 90.9 us -> 87.6 us (0.964)
  Pallas kernels: 84.3 us -> 81 us
    pallas_call x1, Pallas kernels: 84.3 us -> 81 us  [on_device(): pl.pallas_call(kernel, out_shape=jax.ShapeDtypeStruct(velocity.shape, F32...]
where the time goes in v3:
time: 87.6 us; the launch traced here: 87.5 us
  Pallas kernels  81 us (92%)
  matrix products  6.49 us (7%)
    pallas_call x1, Pallas kernels, on_device(): pl.pallas_call(kernel, out_shape=jax.ShapeDtypeStruct(velocity.shape, F32...  81 us
    dot_general x1, matrix products, on_device(): lax.dot_general(home.reshape(-1, width_x), sx, (((1,), (1,)), ((), ())),...  6.49 us

profile of v3, /device:TPU:1, one launch (start us, length us, event | category | flops | bytes accessed | tf_op | source)
XLA Modules:
  0.0 87.5 jit_solution(11389523237992240907)
XLA Ops:
  0.0 81.0 %blocks.1 = f32[3,8,16,1024]{3,2,1,0:T(8,128)} custom-call(f32[3,8,16,1024]{3,2,1,0:T(8,128)} %u_hbm.1, f32[1024,1024]{1,0:T(8,128)} %dx.1, f32[256,256]{1,0:T(8,128)} %dy_hbm.1, f32[128,128]{1,0:T(8,128)} %dz_hbm.1, f32[256,256]{1,0:T(8,128)} %sy_hbm.1, f32[128,128]{1,0:T(8,128)} %sz_hbm.1, f32[72,128]{1,0:T(8,128)} %constant.2.clone.const_hbm), custom_call_target="tpu_custom_call" | custom-call | tf_op jit(solution)/shard_map/blocks/pallas_call | solution.py:778
  81.0 6.5 %fusion = f32[3,8,16,1024]{3,2,1,0:T(8,128)} fusion(f32[3,8,16,1024]{3,2,1,0:T(8,128)} %blocks.1, f32[1024,1024]{1,0:T(8,128)} %param.12), kind=kOutput, calls=%fused_computation | convolution fusion | flops 2415919104 | bytes 7340032 | tf_op jit(solution)/shard_map/dot_general | solution.py:790

commit v4 on v3

--- a/solution.py
+++ b/solution.py
@@ -237,7 +237,12 @@
     sy_hbm,
     sz_hbm,
     const_hbm,
+    sx_hbm,
+    result,
     home,
+    sx,
+    sx_high,
+    sx_low,
     u,
     dy,
     dz,
@@ -350,7 +355,7 @@
         loads.append(
             pltpu.make_async_copy(dx.at[pl.ds(b * 128 + 120, 8), :], dbot.at[b], dma.at[9 + b])
         )
-    pairs = ((u_hbm, u), (const_hbm, const), (dy_hbm, dy), (dz_hbm, dz), (sy_hbm, sy), (sz_hbm, sz))
+    pairs = ((u_hbm, u), (const_hbm, const), (dy_hbm, dy), (dz_hbm, dz), (sy_hbm, sy), (sz_hbm, sz), (sx_hbm, sx))
     for i, (src, dst) in enumerate(pairs):
         loads.append(pltpu.make_async_copy(src, dst, dma.at[17 + i]))
     for load in loads:
@@ -435,6 +440,13 @@
         met_y[...] = metric_rows(dy, first_y, 256, pade_off_diagonal(256)) * 0.1
         met_z[...] = metric_rows(dz, first_z, 128, pade_off_diagonal(128)) * 0.1
 
+    def split_filter():
+        def part(i):
+            rows = pl.ds(i * 16, 16)
+            sx_high[rows, :], sx_low[rows, :] = halves(sx[rows, :])
+
+        each(64, part, 2)
+
     def x_tables():
         unit_x = pade_off_diagonal(1024)
         row, col = iota((128, 128), 0), iota((128, 128), 1)
@@ -696,6 +708,16 @@
                 home[c, i, :, lanes] = value - last * after[i : i + 1]
 
         each(8, one, 2)
+        high, low = halves(home[c].reshape(128, 1024))
+        both = jnp.concatenate([high, low], axis=0)
+
+        def filter_x(j):
+            lanes = pl.ds(pl.multiple_of(j * 256, 256), 256)
+            value = contract(both, sx_high[lanes, :], ((1,), (1,)))
+            value = value[:128] + value[128:] + contract(high, sx_low[lanes, :], ((1,), (1,)))
+            result[c, :, :, lanes] = value.reshape(8, 16, 256)
+
+        each(4, filter_x, 1)
 
     one, two, three = ORDER
     steps = [
@@ -704,6 +726,7 @@
         (derivative_tables,),
         (x_tables,),
         (filter_tables,),
+        (split_filter,),
         (begin_last,),
         (arrive, one),
         (arrive, two),
@@ -760,7 +783,9 @@
         (3, 2, BLK, 128), (3, 2, 8, 1024),
         (NBX, 3, 8, 128), (NBX, 3, 8, 128), (128, 128), (NBX, 8, 1024), (NBX, 8, 1024),
     )
-    scratch = [pltpu.VMEM(s, F32) for s in shapes]
+    scratch = [pltpu.VMEM(velocity.shape, F32), pltpu.VMEM((1024, 1024), F32)]
+    scratch += [pltpu.VMEM((1024, 1024), jnp.bfloat16)] * 2
+    scratch += [pltpu.VMEM(s, F32) for s in shapes]
     scratch += [pltpu.VMEM((256, 256), jnp.bfloat16), pltpu.VMEM((32, 128), jnp.bfloat16)]
     shapes = (
         (256, 128), (256, 128), (4, BLK, 8, 128), (4, BLK, 8, 128),
@@ -770,27 +795,22 @@
     )
     scratch += [pltpu.VMEM(s, F32) for s in shapes]
     counts = (
-        (23,), (6,), (3, 8), (3, 8), (8,), (8,), (4, 3, 2), (4, 3, 2),
+        (24,), (6,), (3, 8), (3, 8), (8,), (8,), (4, 3, 2), (4, 3, 2),
         (2, 3, NBZ), (2, 3, NBZ), (2, 3, NBY), (2, 3, NBY), (3, 8), (3, 8),
         (3, 8), (3, 8),
     )
     scratch += [pltpu.SemaphoreType.DMA(s) for s in counts]
-    home = pl.pallas_call(
+    return pl.pallas_call(
         kernel,
         out_shape=jax.ShapeDtypeStruct(velocity.shape, F32),
-        in_specs=[pl.BlockSpec(memory_space=pl.ANY)] * 7,
+        in_specs=[pl.BlockSpec(memory_space=pl.ANY)] * 8,
         out_specs=vmem,
         scratch_shapes=scratch,
         compiler_params=pltpu.CompilerParams(
             collective_id=1, has_side_effects=True, vmem_limit_bytes=60 * 1024 * 1024
         ),
         name="blocks",
-    )(velocity, dx, dy, dz, sy, sz, jnp.asarray(const))
-    width_x = velocity.shape[3]
-    result = lax.dot_general(
-        home.reshape(-1, width_x), sx, (((1,), (1,)), ((), ())), precision=lax.Precision.HIGH
-    )
-    return result.reshape(velocity.shape)
+    )(velocity, dx, dy, dz, sy, sz, jnp.asarray(const), sx)
 
 
 def solution(mesh):

time: 87.6 us -> 85.7 us (0.978)
  matrix products: 6.49 us -> 0 us
  local copies, waits for them, and re-layouts: 0 us -> 2.73 us
  Pallas kernels: 81 us -> 82.9 us
    dot_general x1 -> x0, matrix products: 6.49 us -> none  [on_device(): lax.dot_general(home.reshape(-1, width_x), sx, (((1,), (1,)), ((), ())),...]
    unnamed x0 -> x1, local copies, waits for them, and re-layouts: none -> 2.73 us
    pallas_call x1, Pallas kernels: 81 us -> 82.9 us  [on_device(): pl.pallas_call(kernel, out_shape=jax.ShapeDtypeStruct(velocity.shape, F32...]
where the time goes in v4:
time: 85.7 us; the launch traced here: 85.6 us
  Pallas kernels  82.9 us (97%)
  local copies, waits for them, and re-layouts  2.73 us (3%)
    pallas_call x1, Pallas kernels, on_device(): pl.pallas_call(kernel, out_shape=jax.ShapeDtypeStruct(velocity.shape, F32...  82.9 us
    unnamed x1, local copies, waits for them, and re-layouts  2.73 us

profile of v4, /device:TPU:1, one launch (start us, length us, event | category | flops | bytes accessed | tf_op | source)
XLA Modules:
  0.0 85.6 jit_solution(17546161158398118566)
XLA Ops:
  0.0 82.9 %blocks.1 = f32[3,8,16,1024]{3,2,1,0:T(8,128)} custom-call(f32[3,8,16,1024]{3,2,1,0:T(8,128)} %u_hbm.1, f32[1024,1024]{1,0:T(8,128)} %dx.1, f32[256,256]{1,0:T(8,128)} %dy_hbm.1, f32[128,128]{1,0:T(8,128)} %dz_hbm.1, f32[256,256]{1,0:T(8,128)} %sy_hbm.1, f32[128,128]{1,0:T(8,128)} %sz_hbm.1, f32[72,128]{1,0:T(8,128)} %constant.2.clone.const_hbm, ...), custom_call_target="tpu_custom_call" | custom-call | tf_op jit(solution)/shard_map/blocks/pallas_call | solution.py:803
  82.9 2.7 %copy.10 = f32[3,8,16,1024]{3,2,1,0:T(8,128)} copy(f32[3,8,16,1024]{3,2,1,0:T(8,128)} %blocks.1) | data formatting | bytes 3145728
